TPU v7x, 32 devices: a whole 2x2x4 slice. The times are simulated.
32 devices in a mesh: row: 4 (over z), col: 4 (over x, core), layer: 2 (over y).
Axes of the slice: x: 2, y: 2, z: 4, core: 2. Of those that a mesh axis runs over, the one named last changes fastest.
Arguments:
- left_blocks: float32 [4, 2, 4, 4, 128, 128], P('row', 'layer', 'col'), may hold values from -1.2 to 1.2
- right_blocks: float32 [2, 4, 4, 8, 128, 128], P('layer', 'row', 'col'), may hold values from -1.2 to 1.2
- pair_stacks: int32 [4, 4, 2, 4, 3, 32], P('row', 'col', 'layer'), may hold values from 0 to 32, as said below
Outputs:
- product_window: float32 [4, 4, 32, 128, 128], P('row', 'col', 'layer')
Inputs may be any that keep to these rules, and one draw needn't show every extreme that they name: `pair_stacks`: entry 0 of a list holds left slots below 4, entry 1 right slots below 8, entry 2 product blocks below 32; the live triples stand first, every other slot holds (0, 0, 32); some list is live in all 32 slots.
All inputs are finite; a program needn't handle non-finite values.
Results may differ from a plain program's by a relative error of at most 0.0003.
Values sent between devices are 32-bit elements; how exact they have to be, the bound alone decides.
A program may use at most 64 MiB of HBM per device.

v0:
```python
import jax
import jax.numpy as jnp
from jax import lax
from jax.sharding import PartitionSpec as P

OUT_TILE = 32


def multiply(running, left_piece, right_piece, left_slot, right_slot, out_slot):
    first_blocks = jnp.take(left_piece, left_slot, axis=0)
    second_blocks = jnp.take(right_piece, right_slot, axis=0)
    products = jnp.einsum(
        "qxy,qyz->qxz",
        first_blocks,
        second_blocks,
        precision=lax.Precision.HIGHEST,
        preferred_element_type=jnp.float32,
    )
    return running.at[out_slot].add(products, mode="drop")


def piece_term(accumulated, left_piece, right_piece, triples):
    left_slot = triples[0]
    right_slot = triples[1]
    out_slot = triples[2]
    return multiply(accumulated, left_piece, right_piece, left_slot, right_slot, out_slot)


def body(left_blocks, right_blocks, pair_stacks):
    left_local = left_blocks[0, 0]
    right_local = right_blocks[0, :, 0]
    stacks = pair_stacks[0, 0, 0]
    block_width = left_local.shape[-1]
    initial = jnp.zeros((OUT_TILE, block_width, block_width), jnp.float32)
    right_whole = lax.all_gather(right_local, "row", axis=0, tiled=True)
    pieces = lax.all_gather(left_local, "col", axis=0, tiled=True)

    def visit(position, running):
        left_piece = lax.dynamic_index_in_dim(pieces, position, 0, keepdims=False)
        right_piece = lax.dynamic_index_in_dim(right_whole, position, 0, keepdims=False)
        triples = lax.dynamic_index_in_dim(stacks, position, 0, keepdims=False)
        return piece_term(running, left_piece, right_piece, triples)

    accumulated = lax.fori_loop(0, pieces.shape[0], visit, initial)
    reduced = lax.psum_scatter(accumulated, "layer", scatter_dimension=0, tiled=True)
    return reduced[None, None]


def solution(mesh):
    placed = (
        P("row", "layer", "col", None, None, None),
        P("layer", "row", "col", None, None, None),
        P("row", "col", "layer", None, None, None),
    )
    return jax.shard_map(
        body,
        mesh=mesh,
        in_specs=placed,
        out_specs=P("row", "col", "layer", None, None),
        check_vma=False,
    )
```

profile of v0, /device:TPU:0, one launch (start us, length us, event | category | flops | bytes accessed | tf_op | source)
XLA Modules:
  0.0 181.9 jit_solution(6074862939140767157)
XLA Ops:
  8.7 19.6 %all-gather.5.cloned.1.call-done = f32[4,1,1,4,128,128]{5,4,3,2,1,0:T(8,128)} async-done(((f32[1,1,1,4,128,128]{5,4,3,2,1,0:T(8,128)}), f32[4,1,1,4,128,128]{5,4,3,2,1,0:T(8,128)}) %all-gather.5.cloned.1.call-update) | async-done | bytes 1048592 | tf_op jit(solution)/shard_map/all_gather | solution.py:36
  28.4 47.5 %all-gather.7.cloned.1.call-done = f32[4,1,1,8,128,128]{5,4,3,2,1,0:T(8,128)} async-done(((f32[1,1,1,8,128,128]{5,4,3,2,1,0:T(8,128)}), f32[4,1,1,8,128,128]{5,4,3,2,1,0:T(8,128)}) %all-gather.7.cloned.1.call-update) | async-done | bytes 2097168 | tf_op jit(solution)/shard_map/all_gather | solution.py:35
  75.9 1.6 broadcast_in_dim.43
  77.5 67.0 %while.13 = (s32[]{:T(128)}, f32[32,128,128]{2,1,0:T(8,128)}, s32[4,3,32]{2,1,0:T(4,128)S(1)}, f32[4,4,128,128]{3,2,1,0:T(8,128)}, f32[4,8,128,128]{3,2,1,0:T(8,128)}, /*index=5*/s32[]{:T(128)}) while((s32[]{:T(128)}, f32[32,128,128]{2,1,0:T(8,128)}, s32[4,3,32]{2,1,0:T(4,128)S(1)}, f32[4,4,128,128]{3,2,1,0:T(8,128)}, ...), condition=%wide.region_2.3_spmd, body=%wide.region_0.2_spmd.sunk | while | flops 806881984 | bytes 22555224 | solution.py:44
  78.5 1.1 dynamic-slice_bitcast_fusion.4
  79.6 2.0 %gather_fusion = f32[32,128,128]{2,1,0:T(8,128)} fusion(f32[8,128,128]{2,1,0:T(8,128)S(1)} %dynamic-slice_bitcast_fusion.4, s32[1024]{0:T(1024)S(1)} %get-tuple-element.158), kind=kCustom, calls=%fused_computation.1.clone.1 | custom fusion | bytes 4194432 | tf_op jit(solution)/shard_map/while/body/eval_jaxpr/jit(_take)/gather | solution.py:11
  81.6 2.0 %gather_fusion.1 = f32[32,128,128]{2,1,0:T(8,128)} fusion(f32[4,128,128]{2,1,0:T(8,128)S(1)} %dynamic-slice_bitcast_fusion.5, s32[1024]{0:T(1024)S(1)} %get-tuple-element.159), kind=kCustom, calls=%fused_computation.clone.1 | custom fusion | bytes 4194432 | tf_op jit(solution)/shard_map/while/body/eval_jaxpr/jit(_take)/gather | solution.py:10
  83.6 4.6 %fusion.17 = f32[32,128,128]{2,1,0:T(8,128)S(1)} fusion(f32[32,128,128]{2,1,0:T(8,128)} %gather_fusion, f32[32,128,128]{2,1,0:T(8,128)} %gather_fusion.1, pred[32]{0:T(512)(128)(4,1)S(1)} %get-tuple-element.160, pred[32]{0:T(512)(128)(4,1)S(1)} %get-tuple-element.161), kind=kOutput, calls=%fused_computation.3.clone.1 | convolution fusion | flops 806354944 | bytes 6291520 | tf_op jit(solution)/shard_map/while/body/eval_jaxpr/qxy,qyz->qxz/dot_general | solution.py:12
  88.2 6.1 %scatter_fusion = f32[32,128,128]{2,1,0:T(8,128)} fusion(f32[32,128,128]{2,1,0:T(8,128)} %get-tuple-element.169, s32[32]{0:T(128)S(1)} %get-tuple-element.155, f32[32,128,128]{2,1,0:T(8,128)S(1)} %fusion.17), kind=kCustom, calls=%fused_computation.2.clone.1 | custom fusion | flops 524288 | bytes 6291584 | tf_op jit(solution)/shard_map/while/body/eval_jaxpr/scatter-add | solution.py:19
  95.4 1.1 dynamic-slice_bitcast_fusion.4
  96.4 2.0 %gather_fusion = f32[32,128,128]{2,1,0:T(8,128)} fusion(f32[8,128,128]{2,1,0:T(8,128)S(1)} %dynamic-slice_bitcast_fusion.4, s32[1024]{0:T(1024)S(1)} %get-tuple-element.158), kind=kCustom, calls=%fused_computation.1.clone.1 | custom fusion | bytes 4194432 | tf_op jit(solution)/shard_map/while/body/eval_jaxpr/jit(_take)/gather | solution.py:11
  98.4 2.0 %gather_fusion.1 = f32[32,128,128]{2,1,0:T(8,128)} fusion(f32[4,128,128]{2,1,0:T(8,128)S(1)} %dynamic-slice_bitcast_fusion.5, s32[1024]{0:T(1024)S(1)} %get-tuple-element.159), kind=kCustom, calls=%fused_computation.clone.1 | custom fusion | bytes 4194432 | tf_op jit(solution)/shard_map/while/body/eval_jaxpr/jit(_take)/gather | solution.py:10
  100.4 4.6 %fusion.17 = f32[32,128,128]{2,1,0:T(8,128)S(1)} fusion(f32[32,128,128]{2,1,0:T(8,128)} %gather_fusion, f32[32,128,128]{2,1,0:T(8,128)} %gather_fusion.1, pred[32]{0:T(512)(128)(4,1)S(1)} %get-tuple-element.160, pred[32]{0:T(512)(128)(4,1)S(1)} %get-tuple-element.161), kind=kOutput, calls=%fused_computation.3.clone.1 | convolution fusion | flops 806354944 | bytes 6291520 | tf_op jit(solution)/shard_map/while/body/eval_jaxpr/qxy,qyz->qxz/dot_general | solution.py:12
  105.0 6.0 %scatter_fusion = f32[32,128,128]{2,1,0:T(8,128)} fusion(f32[32,128,128]{2,1,0:T(8,128)} %get-tuple-element.169, s32[32]{0:T(128)S(1)} %get-tuple-element.155, f32[32,128,128]{2,1,0:T(8,128)S(1)} %fusion.17), kind=kCustom, calls=%fused_computation.2.clone.1 | custom fusion | flops 524288 | bytes 6291584 | tf_op jit(solution)/shard_map/while/body/eval_jaxpr/scatter-add | solution.py:19
  112.1 1.1 dynamic-slice_bitcast_fusion.4
  113.2 2.0 %gather_fusion = f32[32,128,128]{2,1,0:T(8,128)} fusion(f32[8,128,128]{2,1,0:T(8,128)S(1)} %dynamic-slice_bitcast_fusion.4, s32[1024]{0:T(1024)S(1)} %get-tuple-element.158), kind=kCustom, calls=%fused_computation.1.clone.1 | custom fusion | bytes 4194432 | tf_op jit(solution)/shard_map/while/body/eval_jaxpr/jit(_take)/gather | solution.py:11
  115.2 2.0 %gather_fusion.1 = f32[32,128,128]{2,1,0:T(8,128)} fusion(f32[4,128,128]{2,1,0:T(8,128)S(1)} %dynamic-slice_bitcast_fusion.5, s32[1024]{0:T(1024)S(1)} %get-tuple-element.159), kind=kCustom, calls=%fused_computation.clone.1 | custom fusion | bytes 4194432 | tf_op jit(solution)/shard_map/while/body/eval_jaxpr/jit(_take)/gather | solution.py:10
  117.2 4.6 %fusion.17 = f32[32,128,128]{2,1,0:T(8,128)S(1)} fusion(f32[32,128,128]{2,1,0:T(8,128)} %gather_fusion, f32[32,128,128]{2,1,0:T(8,128)} %gather_fusion.1, pred[32]{0:T(512)(128)(4,1)S(1)} %get-tuple-element.160, pred[32]{0:T(512)(128)(4,1)S(1)} %get-tuple-element.161), kind=kOutput, calls=%fused_computation.3.clone.1 | convolution fusion | flops 806354944 | bytes 6291520 | tf_op jit(solution)/shard_map/while/body/eval_jaxpr/qxy,qyz->qxz/dot_general | solution.py:12
  121.7 6.0 %scatter_fusion = f32[32,128,128]{2,1,0:T(8,128)} fusion(f32[32,128,128]{2,1,0:T(8,128)} %get-tuple-element.169, s32[32]{0:T(128)S(1)} %get-tuple-element.155, f32[32,128,128]{2,1,0:T(8,128)S(1)} %fusion.17), kind=kCustom, calls=%fused_computation.2.clone.1 | custom fusion | flops 524288 | bytes 6291584 | tf_op jit(solution)/shard_map/while/body/eval_jaxpr/scatter-add | solution.py:19
  129.9 2.0 %gather_fusion = f32[32,128,128]{2,1,0:T(8,128)} fusion(f32[8,128,128]{2,1,0:T(8,128)S(1)} %dynamic-slice_bitcast_fusion.4, s32[1024]{0:T(1024)S(1)} %get-tuple-element.158), kind=kCustom, calls=%fused_computation.1.clone.1 | custom fusion | bytes 4194432 | tf_op jit(solution)/shard_map/while/body/eval_jaxpr/jit(_take)/gather | solution.py:11
  131.9 2.0 %gather_fusion.1 = f32[32,128,128]{2,1,0:T(8,128)} fusion(f32[4,128,128]{2,1,0:T(8,128)S(1)} %dynamic-slice_bitcast_fusion.5, s32[1024]{0:T(1024)S(1)} %get-tuple-element.159), kind=kCustom, calls=%fused_computation.clone.1 | custom fusion | bytes 4194432 | tf_op jit(solution)/shard_map/while/body/eval_jaxpr/jit(_take)/gather | solution.py:10
  133.9 4.6 %fusion.17 = f32[32,128,128]{2,1,0:T(8,128)S(1)} fusion(f32[32,128,128]{2,1,0:T(8,128)} %gather_fusion, f32[32,128,128]{2,1,0:T(8,128)} %gather_fusion.1, pred[32]{0:T(512)(128)(4,1)S(1)} %get-tuple-element.160, pred[32]{0:T(512)(128)(4,1)S(1)} %get-tuple-element.161), kind=kOutput, calls=%fused_computation.3.clone.1 | convolution fusion | flops 806354944 | bytes 6291520 | tf_op jit(solution)/shard_map/while/body/eval_jaxpr/qxy,qyz->qxz/dot_general | solution.py:12
  138.4 6.1 %scatter_fusion = f32[32,128,128]{2,1,0:T(8,128)} fusion(f32[32,128,128]{2,1,0:T(8,128)} %get-tuple-element.169, s32[32]{0:T(128)S(1)} %get-tuple-element.155, f32[32,128,128]{2,1,0:T(8,128)S(1)} %fusion.17), kind=kCustom, calls=%fused_computation.2.clone.1 | custom fusion | flops 524288 | bytes 6291584 | tf_op jit(solution)/shard_map/while/body/eval_jaxpr/scatter-add | solution.py:19
  144.5 30.9 %reduce-scatter.2.cloned.1.call-done = f32[16,128,128]{2,1,0:T(8,128)} async-done(((f32[32,128,128]{2,1,0:T(8,128)}), f32[16,128,128]{2,1,0:T(8,128)}) %reduce-scatter.2.cloned.1.call-update) | async-done | bytes 1048592 | tf_op jit(solution)/shard_map/reduce_scatter | solution.py:45
  (28 shorter events, 7.3 us)
Async XLA Ops:
  6.5 21.8 %all-gather.5.cloned.1.call-start = ((), (), s32[]{:S(2)}) async-start(), calls=%async_computation.2 | async-start | bytes 1310720 | tf_op jit(solution)/shard_map/all_gather | solution.py:36
  7.3 68.7 %all-gather.7.cloned.1.call-start = ((), (), s32[]{:S(2)}) async-start(), calls=%async_computation.3 | async-start | bytes 2621440 | tf_op jit(solution)/shard_map/all_gather | solution.py:35
  8.0 167.4 %reduce-scatter.2.cloned.1.call-start = ((), (), s32[]{:S(2)}) async-start(), calls=%async_computation.1 | async-start | bytes 3145728 | tf_op jit(solution)/shard_map/reduce_scatter | solution.py:45
Sparse Core Ops, SparseCore 0:
  8.9 19.4 all-gather.4
  29.9 45.9 all-gather.6
  144.7 30.7 reduce-scatter.1
where the time goes:
time: 183 us; the launch traced here: 182 us
  waiting for transfers between devices  99.5 us (54%)
  local copies, waits for them, and re-layouts  26.5 us (14%)
  other arithmetic  24.3 us (13%)
  matrix products  18.2 us (10%)
  between operations  13.1 us (7%)
    all_gather x1, waiting for transfers between devices, body(): right_whole = lax.all_gather(right_local, 'row', axis=0, tiled=True)  47.5 us
    reduce_scatter x1, waiting for transfers between devices, body(): lax.psum_scatter(accumulated, 'layer', scatter_dimension=0, tiled=True)  30.9 us
    scatter-add x4, other arithmetic, multiply(): return running.at[out_slot].add(products, mode='drop')  24.2 us
    all_gather x1, waiting for transfers between devices, body(): pieces = lax.all_gather(left_local, 'col', axis=0, tiled=True)  19.6 us
    dot_general x4, matrix products, multiply(): jnp.einsum('qxy,qyz->qxz', first_blocks, second_blocks, precision=lax.Pre...  18.2 us
    gather x4, local copies, waits for them, and re-layouts, multiply(): first_blocks = jnp.take(left_piece, left_slot, axis=0)  8.03 us
    gather x4, local copies, waits for them, and re-layouts, multiply(): second_blocks = jnp.take(right_piece, right_slot, axis=0)  7.96 us
    squeeze x4, local copies, waits for them, and re-layouts, visit(): lax.dynamic_index_in_dim(right_whole, position, 0, keepdims=False)  4.33 us
  transfers between devices with their start and end apart: 3, of which 3 were waited for; matrix products, arithmetic and copies ran while one was open for 0% of the time, Pallas kernels for 0%

commit v1 on v0

v1 whole, which is shorter than its diff:
```python
import functools

import jax
import jax.numpy as jnp
from jax import lax
from jax.experimental import pallas as pl
from jax.experimental.pallas import tpu as pltpu
from jax.sharding import PartitionSpec as P

OUT_TILE = 32
MESH = pl.DeviceIdType.MESH


def kernel(
    rows, cols, left_ref, right_ref, stacks_ref, out_ref,
    left_all, right_all, lists, tab_v, tab_s, pairs, wide, deep, low, buf,
    ring_send, ring_recv, ly_send, ly_recv, lc_send, lc_recv, st_send, st_recv, tab_sem,
):
    held, sa, bs, _ = left_ref.shape
    sb = right_ref.shape[0]
    half = sb // 2
    pieces, _, cap = stacks_ref.shape
    outs = out_ref.shape[0]
    ring = 2 * rows
    last_send = ring - 2

    row = lax.axis_index("row")
    col = lax.axis_index("col")
    layer = lax.axis_index("layer")
    other = 1 - layer

    def place(layer_at, row_at):
        return jnp.where(layer_at == 0, row_at, ring - 1 - row_at)

    def unplace(spot):
        return jnp.where(spot < rows, 0, 1), jnp.where(spot < rows, spot, ring - 1 - spot)

    def wrap(spot):
        return lax.rem(spot + 2 * ring, ring)

    me = place(layer, row)
    cw_layer, cw_row = unplace(wrap(me + 1))
    cc_layer, cc_row = unplace(wrap(me - 1))
    right_id = {"row": cw_row, "col": col, "layer": cw_layer}
    left_id = {"row": cc_row, "col": col, "layer": cc_layer}
    twin_id = {"row": row, "col": col, "layer": other}

    def peer_id(step):
        return {"row": row, "col": lax.rem(col + step, cols), "layer": layer}

    barrier = pltpu.get_barrier_semaphore()
    for target in (right_id, left_id, twin_id) + tuple(peer_id(j) for j in range(1, cols)):
        pl.semaphore_signal(barrier, inc=1, device_id=target, device_id_type=MESH)
    pl.semaphore_wait(barrier, 3 + cols - 1)

    def remote(src, dst, send, recv, target):
        return pltpu.make_async_remote_copy(
            src_ref=src, dst_ref=dst, send_sem=send, recv_sem=recv,
            device_id=target, device_id_type=MESH)

    def ring_copy(way, step, spot, part, own=False):
        slot = right_all.at[spot, pl.ds(part * half, half)]
        src = right_ref.at[pl.ds(part * half, half)] if own else slot
        return remote(src, slot, ring_send.at[way, step], ring_recv.at[way, step],
                      right_id if way == 0 else left_id)

    def send_ring(step, own=False):
        part = lax.rem(step, 2)
        ring_copy(0, step, wrap(me - step // 2), part, own).start()
        ring_copy(1, step, wrap(me + step // 2), 1 - part, own).start()

    def await_ring(step):
        part = lax.rem(step, 2)
        ring_copy(0, step, wrap(me - 1 - step // 2), part).wait_recv()
        ring_copy(1, step, wrap(me + 1 + step // 2), 1 - part).wait_recv()

    stack_copy = remote(stacks_ref, lists.at[layer], st_send, st_recv, twin_id)
    stack_copy.start()

    def twin_copy(i):
        return remote(left_ref.at[i], left_all.at[layer, col * held + i],
                      ly_send.at[i], ly_recv.at[i], twin_id)

    def twin_arrival(i):
        return remote(left_ref.at[i], left_all.at[other, col * held + i],
                      ly_send.at[i], ly_recv.at[i], twin_id)

    def peer_copy(kind, i, j):
        at = (layer if kind == 0 else other), col * held + i
        src = left_ref.at[i] if kind == 0 else left_all.at[at]
        return remote(src, left_all.at[at], lc_send.at[kind, i, j - 1], lc_recv.at[kind, i, j - 1], peer_id(j))

    def peer_arrival(kind, i, j):
        at = (layer if kind == 0 else other), lax.rem(col - j + cols, cols) * held + i
        return remote(left_all.at[at], left_all.at[at], lc_send.at[kind, i, j - 1],
                      lc_recv.at[kind, i, j - 1], peer_id(j))

    for i in range(held):
        twin_copy(i).start()
    send_ring(0, True)
    for i in range(held):
        for j in range(1, cols):
            peer_copy(0, i, j).start()
    send_ring(1, True)

    lists[layer] = stacks_ref[...]
    for i in range(held):
        left_all[layer, col * held + i] = left_ref[i]
    right_all[me] = right_ref[...]
    for o in range(outs + 1):
        buf[cap + o] = jnp.zeros((bs, bs), jnp.float32)

    remote(stacks_ref, lists.at[other], st_send, st_recv, twin_id).wait_recv()

    def gathered(entry):
        return jnp.concatenate(
            [lists[t // pieces, t % pieces, entry:entry + 1, :] for t in range(2 * pieces)], axis=0)

    out_at = gathered(2) - layer * outs
    out_at = jnp.where((out_at >= 0) & (out_at < outs), out_at, outs)
    lane = lax.broadcasted_iota(jnp.int32, out_at.shape, 1)
    before = cap + out_at
    final = cap + jnp.minimum(lane, outs)
    for q in range(cap):
        mine = out_at[:, q:q + 1]
        before = jnp.where((out_at == mine) & (lane > q), q, before)
        final = jnp.where(lane == mine, q, final)
    tab_v[0, :, :cap] = gathered(1) * sa + gathered(0)
    tab_v[1, :, :cap] = before
    tab_v[2, :, :cap] = final
    tab_copy = pltpu.make_async_copy(tab_v, tab_s, tab_sem)
    tab_copy.start()

    for i in range(held):
        twin_arrival(i).wait_recv()
        for j in range(1, cols):
            peer_copy(1, i, j).start()
    tab_copy.wait()

    def split(value):
        high = value.astype(jnp.bfloat16)
        return high, (value - high.astype(jnp.float32)).astype(jnp.bfloat16)

    def accumulate(spot, last=False):
        layer_at, row_at = unplace(spot)
        at = layer_at * pieces + row_at
        for a in range(sa):
            high, rest = split(left_all[layer_at, row_at, a])
            wide[a * bs:(a + 1) * bs, :bs] = high
            wide[a * bs:(a + 1) * bs, bs:] = rest
        for b in range(0, sb, 2):
            for n in range(2):
                high, rest = split(right_all[spot, b + n])
                for m in range(2):
                    deep[m * bs:(m + 1) * bs, n * bs:(n + 1) * bs] = high
                    low[m * bs:(m + 1) * bs, n * bs:(n + 1) * bs] = rest
            product = jnp.dot(wide[...], deep[...], preferred_element_type=jnp.float32)
            product += jnp.dot(wide[...], low[...], preferred_element_type=jnp.float32)
            for n in range(2):
                for a in range(sa):
                    pairs[(b + n) * sa + a] = product[a * bs:(a + 1) * bs, n * bs:(n + 1) * bs]

        def chain(q, carry):
            buf[q] = pairs[tab_s[0, at, q]] + buf[tab_s[1, at, q]]
            return carry

        lax.fori_loop(0, cap, chain, 0)

        def keep(o, carry):
            if last:
                out_ref[o] = buf[tab_s[2, at, o]]
            else:
                buf[cap + o] = buf[tab_s[2, at, o]]
            return carry

        lax.fori_loop(0, outs, keep, 0)

    def advance(d):
        await_ring(2 * d - 2)
        send_ring(2 * d)
        await_ring(2 * d - 1)

        @pl.when(2 * d + 1 <= last_send)
        def _():
            send_ring(2 * d + 1)

    advance(1)
    for kind in range(2):
        for i in range(held):
            for j in range(1, cols):
                peer_arrival(kind, i, j).wait_recv()

    def first(j, carry):
        accumulate(wrap(me + j - 1))
        return carry

    lax.fori_loop(0, 3, first, 0)

    def step(d, carry):
        advance(d)

        def side(j, inner):
            accumulate(wrap(me + (2 * j - 1) * d))
            return inner

        lax.fori_loop(0, 2, side, 0)
        return carry

    lax.fori_loop(2, rows, step, 0)
    await_ring(last_send)
    accumulate(wrap(me + rows), True)

    stack_copy.wait_send()
    for i in range(held):
        twin_copy(i).wait_send()
        for kind in range(2):
            for j in range(1, cols):
                peer_copy(kind, i, j).wait_send()

    def drain(s, carry):
        part = lax.rem(s, 2)
        ring_copy(0, s, wrap(me - s // 2), part).wait_send()
        ring_copy(1, s, wrap(me + s // 2), 1 - part).wait_send()
        return carry

    lax.fori_loop(0, last_send + 1, drain, 0)


def body(rows, cols, left_blocks, right_blocks, pair_stacks):
    left_local = left_blocks[0, 0]
    right_local = right_blocks[0, 0, 0]
    stacks = pair_stacks[0, 0, 0]
    held, sa, bs, _ = left_local.shape
    sb = right_local.shape[0]
    pieces, _, cap = stacks.shape
    outs = OUT_TILE // 2
    f32 = jnp.float32
    dma = pltpu.SemaphoreType.DMA
    vmem = pl.BlockSpec(memory_space=pltpu.VMEM)
    block = bs * bs * 4
    blocks = 2 * pieces * (sa + sb) + sa * sb + cap + 2 * outs + sb + held * sa + 16
    result = pl.pallas_call(
        functools.partial(kernel, rows, cols),
        out_shape=jax.ShapeDtypeStruct((outs, bs, bs), f32),
        in_specs=[vmem] * 3,
        out_specs=vmem,
        scratch_shapes=[
            pltpu.VMEM((2, pieces, sa, bs, bs), f32),
            pltpu.VMEM((2 * rows, sb, bs, bs), f32),
            pltpu.VMEM((2, pieces, 3, cap), jnp.int32),
            pltpu.VMEM((3, 2 * pieces, 128), jnp.int32),
            pltpu.SMEM((3, 2 * pieces, 128), jnp.int32),
            pltpu.VMEM((sa * sb, bs, bs), f32),
            pltpu.VMEM((sa * bs, 2 * bs), jnp.bfloat16),
            pltpu.VMEM((2 * bs, 2 * bs), jnp.bfloat16),
            pltpu.VMEM((2 * bs, 2 * bs), jnp.bfloat16),
            pltpu.VMEM((cap + outs + 1, bs, bs), f32),
            dma((2, 2 * rows - 1)),
            dma((2, 2 * rows - 1)),
            dma((held,)),
            dma((held,)),
            dma((2, held, cols - 1)),
            dma((2, held, cols - 1)),
            dma, dma, dma,
        ],
        compiler_params=pltpu.CompilerParams(
            collective_id=0, has_side_effects=True, vmem_limit_bytes=blocks * block + (6 << 20)),
        name="ring_window",
    )(left_local, right_local, stacks)
    return result[None, None]


def solution(mesh):
    placed = (
        P("row", "layer", "col", None, None, None),
        P("layer", "row", "col", None, None, None),
        P("row", "col", "layer", None, None, None),
    )
    return jax.shard_map(
        functools.partial(body, mesh.shape["row"], mesh.shape["col"]),
        mesh=mesh,
        in_specs=placed,
        out_specs=P("row", "col", "layer", None, None),
        check_vma=False,
    )
```

time: 183 us -> 55.8 us (0.30)
  waiting for transfers between devices: 99.5 us -> 0 us
  Pallas kernels: 0 us -> 51.5 us
  other arithmetic: 24.3 us -> 0 us
  local copies, waits for them, and re-layouts: 26.5 us -> 3.66 us
  matrix products: 18.2 us -> 0 us
  between operations: 13.1 us -> 0.01 us
    all_gather x2 -> x0, waiting for transfers between devices: 67.2 us -> none  [the longest x1 47.5 us: body(): right_whole = lax.all_gather(right_local, 'row', axis=0, tiled=True)]
    pallas_call x0 -> x1, Pallas kernels: none -> 51.5 us  [body(): pl.pallas_call(functools.partial(kernel, rows, cols), out_shape=jax.Shape...]
    reduce_scatter x1 -> x0, waiting for transfers between devices: 30.9 us -> none  [body(): lax.psum_scatter(accumulated, 'layer', scatter_dimension=0, tiled=True)]
    scatter-add x4 -> x0, other arithmetic: 24.2 us -> none  [multiply(): return running.at[out_slot].add(products, mode='drop')]
    dot_general x4 -> x0, matrix products: 18.2 us -> none  [multiply(): jnp.einsum('qxy,qyz->qxz', first_blocks, second_blocks, precision=lax.Pre...]
    gather x8 -> x0, local copies, waits for them, and re-layouts: 16 us -> none  [the longest x4 8.03 us: multiply(): first_blocks = jnp.take(left_piece, left_slot, axis=0)]
    squeeze x8 -> x0, local copies, waits for them, and re-layouts: 8.23 us -> none  [the longest x4 4.33 us: visit(): lax.dynamic_index_in_dim(right_whole, position, 0, keepdims=False)]
    unnamed x1 -> x6, local copies, waits for them, and re-layouts: 0.7 us -> 3.66 us
  transfers between devices with their start and end apart: 3 -> 0, of which waited for: 3 -> 0; matrix products, arithmetic and copies ran while one was open for 0% -> 0% of each run, Pallas kernels for 0% -> 0%
where the time goes in v1:
time: 55.8 us; the launch traced here: 55.2 us
  Pallas kernels  51.5 us (92%)
  local copies, waits for them, and re-layouts  3.66 us (7%)
    pallas_call x1, Pallas kernels, body(): pl.pallas_call(functools.partial(kernel, rows, cols), out_shape=jax.Shape...  51.5 us
    unnamed x6, local copies, waits for them, and re-layouts  3.66 us

profile of v1, /device:TPU:0, one launch (start us, length us, event | category | flops | bytes accessed | tf_op | source)
XLA Modules:
  0.0 55.2 jit_solution(4519188058451860081)
XLA Ops:
  0.0 0.7 %copy.6 = s32[1,1,1,4,3,32]{5,4,3,2,1,0:T(4,128)S(1)} copy(s32[1,1,1,4,3,32]{5,3,4,2,1,0:T(4,128)} %param.5) | data formatting | bytes 3072 | tf_op args[2]
  0.7 0.0 copy-start
  0.7 1.0 %copy-done = f32[1,1,1,8,128,128]{5,4,3,2,1,0:T(8,128)S(1)} copy-done((f32[1,1,1,8,128,128]{5,4,3,2,1,0:T(8,128)S(1)}, f32[1,1,1,8,128,128]{5,4,3,2,1,0:T(8,128)}, u32[]{:S(2)}) %copy-start) | copy-done | bytes 524312
  1.7 0.0 copy-start.1
  1.7 0.9 %copy-done.1 = f32[1,1,1,4,128,128]{5,4,3,2,1,0:T(8,128)S(1)} copy-done((f32[1,1,1,4,128,128]{5,4,3,2,1,0:T(8,128)S(1)}, f32[1,1,1,4,128,128]{5,4,3,2,1,0:T(8,128)}, u32[]{:S(2)}) %copy-start.1) | copy-done | bytes 262168
  2.7 51.5 %ring_window.1 = f32[16,128,128]{2,1,0:T(8,128)S(1)} custom-call(f32[1,4,128,128]{3,2,1,0:T(8,128)S(1)} %bitcast.8, f32[8,128,128]{2,1,0:T(8,128)S(1)} %bitcast.7, s32[4,3,32]{2,1,0:T(4,128)S(1)} %bitcast.9), custom_call_target="tpu_custom_call" | custom-call | tf_op jit(solution)/shard_map/ring_window/pallas_call | solution.py:242
  54.2 1.0 %copy.8 = f32[1,1,16,128,128]{4,3,2,1,0:T(8,128)} copy(f32[1,1,16,128,128]{4,3,2,1,0:T(8,128)S(1)} %bitcast.6) | data formatting | bytes 2097152
Async XLA Ops:
  0.7 1.0 %copy-start = (f32[1,1,1,8,128,128]{5,4,3,2,1,0:T(8,128)S(1)}, f32[1,1,1,8,128,128]{5,4,3,2,1,0:T(8,128)}, u32[]{:S(2)}) copy-start(f32[1,1,1,8,128,128]{5,4,3,2,1,0:T(8,128)} %param.4) | copy-start | bytes 1572868
  1.7 0.9 %copy-start.1 = (f32[1,1,1,4,128,128]{5,4,3,2,1,0:T(8,128)S(1)}, f32[1,1,1,4,128,128]{5,4,3,2,1,0:T(8,128)}, u32[]{:S(2)}) copy-start(f32[1,1,1,4,128,128]{5,4,3,2,1,0:T(8,128)} %param.3) | copy-start | bytes 786436

commit v2 on v1

--- a/solution.py
+++ b/solution.py
@@ -14,15 +14,16 @@
 def kernel(
     rows, cols, left_ref, right_ref, stacks_ref, out_ref,
     left_all, right_all, lists, tab_v, tab_s, pairs, wide, deep, low, buf,
-    ring_send, ring_recv, ly_send, ly_recv, lc_send, lc_recv, st_send, st_recv, tab_sem,
+    ring_send, ring_recv, end_send, end_recv, ly_send, ly_recv, lc_send, lc_recv,
+    st_send, st_recv, tab_sem, own_sem,
 ):
     held, sa, bs, _ = left_ref.shape
     sb = right_ref.shape[0]
     half = sb // 2
-    pieces, _, cap = stacks_ref.shape
+    _, pieces, cap = stacks_ref.shape
     outs = out_ref.shape[0]
     ring = 2 * rows
-    last_send = ring - 2
+    quarter = sb // 4
 
     row = lax.axis_index("row")
     col = lax.axis_index("col")
@@ -51,6 +52,14 @@
     barrier = pltpu.get_barrier_semaphore()
     for target in (right_id, left_id, twin_id) + tuple(peer_id(j) for j in range(1, cols)):
         pl.semaphore_signal(barrier, inc=1, device_id=target, device_id_type=MESH)
+
+    own_copies = [
+        pltpu.make_async_copy(right_ref, right_all.at[me], own_sem.at[0]),
+        pltpu.make_async_copy(left_ref, left_all.at[layer, pl.ds(col * held, held)], own_sem.at[1]),
+        pltpu.make_async_copy(stacks_ref, lists.at[layer], own_sem.at[2]),
+    ]
+    for copy in own_copies:
+        copy.start()
     pl.semaphore_wait(barrier, 3 + cols - 1)
 
     def remote(src, dst, send, recv, target):
@@ -73,6 +82,28 @@
         part = lax.rem(step, 2)
         ring_copy(0, step, wrap(me - 1 - step // 2), part).wait_recv()
         ring_copy(1, step, wrap(me + 1 + step // 2), 1 - part).wait_recv()
+
+    def by_cw(spot):
+        by_layer = (spot == 0) | (spot == rows)
+        by_row = (spot == rows - 1) | (spot == ring - 1)
+        return jnp.where(by_layer, 1, jnp.where(by_row, 3, 2))
+
+    def end_copy(way, t):
+        spot = wrap(me - (rows - 1)) if way == 0 else wrap(me + rows - 1)
+        slot = right_all.at[spot, pl.ds(t * quarter, quarter)]
+        return remote(slot, slot, end_send.at[way, t], end_recv.at[t], right_id if way == 0 else left_id)
+
+    cw_count, cc_count = by_cw(wrap(me + 1)), by_cw(wrap(me - 1))
+
+    def ends(way, t, action):
+        @pl.when(t < cw_count if way == 0 else t >= cc_count)
+        def _():
+            copy = end_copy(way, t)
+            copy.start() if action == "start" else copy.wait_send()
+
+    def await_end(t):
+        slot = right_all.at[wrap(me + rows), pl.ds(t * quarter, quarter)]
+        remote(slot, slot, end_send.at[0, t], end_recv.at[t], right_id).wait_recv()
 
     stack_copy = remote(stacks_ref, lists.at[layer], st_send, st_recv, twin_id)
     stack_copy.start()
@@ -103,18 +134,15 @@
             peer_copy(0, i, j).start()
     send_ring(1, True)
 
-    lists[layer] = stacks_ref[...]
-    for i in range(held):
-        left_all[layer, col * held + i] = left_ref[i]
-    right_all[me] = right_ref[...]
     for o in range(outs + 1):
         buf[cap + o] = jnp.zeros((bs, bs), jnp.float32)
 
+    for copy in own_copies:
+        copy.wait()
     remote(stacks_ref, lists.at[other], st_send, st_recv, twin_id).wait_recv()
 
     def gathered(entry):
-        return jnp.concatenate(
-            [lists[t // pieces, t % pieces, entry:entry + 1, :] for t in range(2 * pieces)], axis=0)
+        return jnp.concatenate([lists[0, entry], lists[1, entry]], axis=0)
 
     out_at = gathered(2) - layer * outs
     out_at = jnp.where((out_at >= 0) & (out_at < outs), out_at, outs)
@@ -141,48 +169,70 @@
         high = value.astype(jnp.bfloat16)
         return high, (value - high.astype(jnp.float32)).astype(jnp.bfloat16)
 
-    def accumulate(spot, last=False):
+    def widen(spot):
         layer_at, row_at = unplace(spot)
-        at = layer_at * pieces + row_at
         for a in range(sa):
             high, rest = split(left_all[layer_at, row_at, a])
             wide[a * bs:(a + 1) * bs, :bs] = high
             wide[a * bs:(a + 1) * bs, bs:] = rest
-        for b in range(0, sb, 2):
-            for n in range(2):
-                high, rest = split(right_all[spot, b + n])
-                for m in range(2):
-                    deep[m * bs:(m + 1) * bs, n * bs:(n + 1) * bs] = high
-                    low[m * bs:(m + 1) * bs, n * bs:(n + 1) * bs] = rest
-            product = jnp.dot(wide[...], deep[...], preferred_element_type=jnp.float32)
-            product += jnp.dot(wide[...], low[...], preferred_element_type=jnp.float32)
-            for n in range(2):
-                for a in range(sa):
-                    pairs[(b + n) * sa + a] = product[a * bs:(a + 1) * bs, n * bs:(n + 1) * bs]
+
+    def multiply(spot, b):
+        for n in range(2):
+            high, rest = split(right_all[spot, b + n])
+            for m in range(2):
+                deep[m * bs:(m + 1) * bs, n * bs:(n + 1) * bs] = high
+                low[m * bs:(m + 1) * bs, n * bs:(n + 1) * bs] = rest
+        product = jnp.dot(wide[...], deep[...], preferred_element_type=jnp.float32)
+        product += jnp.dot(wide[...], low[...], preferred_element_type=jnp.float32)
+        for n in range(2):
+            for a in range(sa):
+                pairs[(b + n) * sa + a] = product[a * bs:(a + 1) * bs, n * bs:(n + 1) * bs]
+
+    def gather_sums(spot, target, offset):
+        layer_at, row_at = unplace(spot)
+        at = layer_at * pieces + row_at
 
         def chain(q, carry):
             buf[q] = pairs[tab_s[0, at, q]] + buf[tab_s[1, at, q]]
             return carry
 
-        lax.fori_loop(0, cap, chain, 0)
+        lax.fori_loop(0, cap, chain, 0, unroll=4)
 
         def keep(o, carry):
-            if last:
-                out_ref[o] = buf[tab_s[2, at, o]]
-            else:
-                buf[cap + o] = buf[tab_s[2, at, o]]
+            target[offset + o] = buf[tab_s[2, at, o]]
             return carry
 
-        lax.fori_loop(0, outs, keep, 0)
+        lax.fori_loop(0, outs, keep, 0, unroll=4)
+
+    def accumulate(spot):
+        widen(spot)
+        for b in range(0, sb, 2):
+            multiply(spot, b)
+        gather_sums(spot, buf, cap)
 
     def advance(d):
         await_ring(2 * d - 2)
-        send_ring(2 * d)
+
+        @pl.when(d < rows - 1)
+        def _():
+            send_ring(2 * d)
+
+        @pl.when(d == rows - 1)
+        def _():
+            for t in range(2):
+                ends(0, t, "start")
+                ends(1, 3 - t, "start")
+
         await_ring(2 * d - 1)
 
-        @pl.when(2 * d + 1 <= last_send)
+        @pl.when(d < rows - 1)
         def _():
             send_ring(2 * d + 1)
+
+        @pl.when(d == rows - 1)
+        def _():
+            ends(0, 2, "start")
+            ends(1, 1, "start")
 
     advance(1)
     for kind in range(2):
@@ -207,9 +257,8 @@
         return carry
 
     lax.fori_loop(2, rows, step, 0)
-    await_ring(last_send)
-    accumulate(wrap(me + rows), True)
-
+    opposite = wrap(me + rows)
+    widen(opposite)
     stack_copy.wait_send()
     for i in range(held):
         twin_copy(i).wait_send()
@@ -223,16 +272,24 @@
         ring_copy(1, s, wrap(me + s // 2), 1 - part).wait_send()
         return carry
 
-    lax.fori_loop(0, last_send + 1, drain, 0)
+    lax.fori_loop(0, ring - 2, drain, 0)
+    for t in (0, 3, 1, 2):
+        await_end(t)
+        for b in range(t * quarter, (t + 1) * quarter, 2):
+            multiply(opposite, b)
+    gather_sums(opposite, out_ref, 0)
+    for t in range(3):
+        ends(0, t, "wait")
+        ends(1, 3 - t, "wait")
 
 
 def body(rows, cols, left_blocks, right_blocks, pair_stacks):
     left_local = left_blocks[0, 0]
     right_local = right_blocks[0, 0, 0]
-    stacks = pair_stacks[0, 0, 0]
+    stacks = jnp.swapaxes(pair_stacks[0, 0, 0], 0, 1)
     held, sa, bs, _ = left_local.shape
     sb = right_local.shape[0]
-    pieces, _, cap = stacks.shape
+    _, pieces, cap = stacks.shape
     outs = OUT_TILE // 2
     f32 = jnp.float32
     dma = pltpu.SemaphoreType.DMA
@@ -242,12 +299,12 @@
     result = pl.pallas_call(
         functools.partial(kernel, rows, cols),
         out_shape=jax.ShapeDtypeStruct((outs, bs, bs), f32),
-        in_specs=[vmem] * 3,
+        in_specs=[pl.BlockSpec(memory_space=pltpu.HBM)] * 3,
         out_specs=vmem,
         scratch_shapes=[
             pltpu.VMEM((2, pieces, sa, bs, bs), f32),
             pltpu.VMEM((2 * rows, sb, bs, bs), f32),
-            pltpu.VMEM((2, pieces, 3, cap), jnp.int32),
+            pltpu.VMEM((2, 3, pieces, cap), jnp.int32),
             pltpu.VMEM((3, 2 * pieces, 128), jnp.int32),
             pltpu.SMEM((3, 2 * pieces, 128), jnp.int32),
             pltpu.VMEM((sa * sb, bs, bs), f32),
@@ -255,13 +312,16 @@
             pltpu.VMEM((2 * bs, 2 * bs), jnp.bfloat16),
             pltpu.VMEM((2 * bs, 2 * bs), jnp.bfloat16),
             pltpu.VMEM((cap + outs + 1, bs, bs), f32),
-            dma((2, 2 * rows - 1)),
-            dma((2, 2 * rows - 1)),
+            dma((2, 2 * rows - 2)),
+            dma((2, 2 * rows - 2)),
+            dma((2, 4)),
+            dma((4,)),
             dma((held,)),
             dma((held,)),
             dma((2, held, cols - 1)),
             dma((2, held, cols - 1)),
             dma, dma, dma,
+            dma((3,)),
         ],
         compiler_params=pltpu.CompilerParams(
             collective_id=0, has_side_effects=True, vmem_limit_bytes=blocks * block + (6 << 20)),

time: 55.8 us -> 54.7 us (0.980)
  Pallas kernels: 51.5 us -> 50.2 us
    pallas_call x1, Pallas kernels: 51.5 us -> 50.2 us  [body(): pl.pallas_call(functools.partial(kernel, rows, cols), out_shape=jax.Shape...]
    unnamed x6 -> x7, local copies, waits for them, and re-layouts: 3.66 us -> 3.65 us
where the time goes in v2:
time: 54.7 us; the launch traced here: 53.9 us
  Pallas kernels  50.2 us (92%)
  local copies, waits for them, and re-layouts  3.65 us (7%)
    pallas_call x1, Pallas kernels, body(): pl.pallas_call(functools.partial(kernel, rows, cols), out_shape=jax.Shape...  50.2 us
    unnamed x7, local copies, waits for them, and re-layouts  3.65 us

profile of v2, /device:TPU:0, one launch (start us, length us, event | category | flops | bytes accessed | tf_op | source)
XLA Modules:
  0.0 53.9 jit_solution(17778200336134160383)
XLA Ops:
  0.0 0.0 copy-start
  0.0 1.0 %copy-done = f32[1,1,1,8,128,128]{5,4,3,2,1,0:T(8,128)S(1)} copy-done((f32[1,1,1,8,128,128]{5,4,3,2,1,0:T(8,128)S(1)}, f32[1,1,1,8,128,128]{5,4,3,2,1,0:T(8,128)}, u32[]{:S(2)}) %copy-start) | copy-done | bytes 524312
  1.0 0.0 copy-start.1
  1.0 0.9 %copy-done.1 = f32[1,1,1,4,128,128]{5,4,3,2,1,0:T(8,128)S(1)} copy-done((f32[1,1,1,4,128,128]{5,4,3,2,1,0:T(8,128)S(1)}, f32[1,1,1,4,128,128]{5,4,3,2,1,0:T(8,128)}, u32[]{:S(2)}) %copy-start.1) | copy-done | bytes 262168
  2.0 0.0 copy-start.2
  2.0 0.7 %copy-done.2 = s32[1,1,1,4,3,32]{5,3,4,2,1,0:T(4,128)S(1)} copy-done((s32[1,1,1,4,3,32]{5,3,4,2,1,0:T(4,128)S(1)}, s32[1,1,1,4,3,32]{5,3,4,2,1,0:T(4,128)}, u32[]{:S(2)}) %copy-start.2) | copy-done | bytes 1560
  2.7 50.2 %ring_window.1 = f32[16,128,128]{2,1,0:T(8,128)S(1)} custom-call(f32[1,4,128,128]{3,2,1,0:T(8,128)S(1)} %bitcast.8, f32[8,128,128]{2,1,0:T(8,128)S(1)} %bitcast.7, s32[3,4,32]{2,1,0:T(4,128)S(1)} %bitcast.9), custom_call_target="tpu_custom_call" | custom-call | tf_op jit(solution)/shard_map/ring_window/pallas_call | solution.py:299
  52.9 1.0 %copy.5 = f32[1,1,16,128,128]{4,3,2,1,0:T(8,128)} copy(f32[1,1,16,128,128]{4,3,2,1,0:T(8,128)S(1)} %bitcast.6) | data formatting | bytes 2097152
Async XLA Ops:
  0.0 1.0 %copy-start = (f32[1,1,1,8,128,128]{5,4,3,2,1,0:T(8,128)S(1)}, f32[1,1,1,8,128,128]{5,4,3,2,1,0:T(8,128)}, u32[]{:S(2)}) copy-start(f32[1,1,1,8,128,128]{5,4,3,2,1,0:T(8,128)} %param.4) | copy-start | bytes 1572868
  1.0 0.9 %copy-start.1 = (f32[1,1,1,4,128,128]{5,4,3,2,1,0:T(8,128)S(1)}, f32[1,1,1,4,128,128]{5,4,3,2,1,0:T(8,128)}, u32[]{:S(2)}) copy-start(f32[1,1,1,4,128,128]{5,4,3,2,1,0:T(8,128)} %param.3) | copy-start | bytes 786436
  2.0 0.7 %copy-start.2 = (s32[1,1,1,4,3,32]{5,3,4,2,1,0:T(4,128)S(1)}, s32[1,1,1,4,3,32]{5,3,4,2,1,0:T(4,128)}, u32[]{:S(2)}) copy-start(s32[1,1,1,4,3,32]{5,3,4,2,1,0:T(4,128)} %param.5) | copy-start | bytes 4612

commit v3 on v2

v3 whole, which is shorter than its diff:
```python
import functools

import jax
import jax.numpy as jnp
from jax import lax
from jax.experimental import pallas as pl
from jax.experimental.pallas import tpu as pltpu
from jax.sharding import PartitionSpec as P

OUT_TILE = 32
MESH = pl.DeviceIdType.MESH


def kernel(
    rows, cols, left_ref, right_ref, stacks_ref, out_ref,
    left_all, right_all, lists, tab_v, tab_s, pairs, wide, buf,
    ring_send, ring_recv, end_send, end_recv, ly_send, ly_recv, lc_send, lc_recv,
    st_send, st_recv, tab_sem, own_sem,
):
    held, sa, bs, _ = left_ref.shape
    sb = right_ref.shape[0]
    half = sb // 2
    _, pieces, cap = stacks_ref.shape
    outs = out_ref.shape[0]
    ring = 2 * rows
    quarter = sb // 4

    row = lax.axis_index("row")
    col = lax.axis_index("col")
    layer = lax.axis_index("layer")
    other = 1 - layer

    def place(layer_at, row_at):
        return jnp.where(layer_at == 0, row_at, ring - 1 - row_at)

    def unplace(spot):
        return jnp.where(spot < rows, 0, 1), jnp.where(spot < rows, spot, ring - 1 - spot)

    def wrap(spot):
        return lax.rem(spot + 2 * ring, ring)

    me = place(layer, row)
    cw_layer, cw_row = unplace(wrap(me + 1))
    cc_layer, cc_row = unplace(wrap(me - 1))
    right_id = {"row": cw_row, "col": col, "layer": cw_layer}
    left_id = {"row": cc_row, "col": col, "layer": cc_layer}
    twin_id = {"row": row, "col": col, "layer": other}

    chips = cols // 2
    sibling = col + 1 - 2 * lax.rem(col, 2)
    sibling_id = {"row": row, "col": sibling, "layer": layer}

    def peer_col(step):
        return lax.rem(col + 2 * step, cols)

    def peer_id(step):
        return {"row": row, "col": peer_col(step), "layer": layer}

    barrier = pltpu.get_barrier_semaphore()
    for target in (right_id, left_id, twin_id, sibling_id) + tuple(peer_id(j) for j in range(1, chips)):
        pl.semaphore_signal(barrier, inc=1, device_id=target, device_id_type=MESH)

    own_copies = [
        pltpu.make_async_copy(right_ref, right_all.at[me], own_sem.at[0]),
        pltpu.make_async_copy(left_ref, left_all.at[layer, pl.ds(col * held, held)], own_sem.at[1]),
        pltpu.make_async_copy(stacks_ref, lists.at[layer], own_sem.at[2]),
    ]
    for copy in own_copies:
        copy.start()
    pl.semaphore_wait(barrier, 3 + chips)

    def remote(src, dst, send, recv, target):
        return pltpu.make_async_remote_copy(
            src_ref=src, dst_ref=dst, send_sem=send, recv_sem=recv,
            device_id=target, device_id_type=MESH)

    def pick(way, ahead, back):
        return jnp.where(way == 0, ahead, back)

    def toward(way):
        return {"row": pick(way, cw_row, cc_row), "col": col, "layer": pick(way, cw_layer, cc_layer)}

    def ring_copy(way, step, away, own=False):
        spot = wrap(me - (1 - 2 * way) * away)
        part = pick(way, lax.rem(step, 2), 1 - lax.rem(step, 2))
        slot = right_all.at[spot, pl.ds(part * half, half)]
        src = right_ref.at[pl.ds(part * half, half)] if own else slot
        return remote(src, slot, ring_send.at[way, step], ring_recv.at[way, step], toward(way))

    first_way = jnp.where((me == 0) | (me == rows), 1, 0)
    ways = (first_way, 1 - first_way)

    def send_ring(way, step, own=False):
        ring_copy(way, step, step // 2, own).start()

    def await_ring(way, step):
        ring_copy(way, step, 1 + step // 2).wait_recv()

    def by_cw(spot):
        by_layer = (spot == 0) | (spot == rows)
        by_row = (spot == rows - 1) | (spot == ring - 1)
        return jnp.where(by_layer, 1, jnp.where(by_row, 3, 2))

    cw_count, cc_count = by_cw(wrap(me + 1)), 4 - by_cw(wrap(me - 1))

    def end_copy(way, u):
        t = pick(way, u, 3 - u)
        slot = right_all.at[wrap(me - (1 - 2 * way) * (rows - 1)), pl.ds(t * quarter, quarter)]
        return remote(slot, slot, end_send.at[way, t], end_recv.at[t], toward(way))

    def send_end(way, u):
        @pl.when(u < pick(way, cw_count, cc_count))
        def _():
            end_copy(way, u).start()

    def drain_end(way, u):
        @pl.when(u < pick(way, cw_count, cc_count))
        def _():
            end_copy(way, u).wait_send()

    def await_end(t):
        slot = right_all.at[wrap(me + rows), pl.ds(t * quarter, quarter)]
        remote(slot, slot, end_send.at[0, t], end_recv.at[t], right_id).wait_recv()

    stack_copy = remote(stacks_ref, lists.at[layer], st_send, st_recv, twin_id)
    stack_copy.start()

    def twin_copy(i):
        return remote(left_ref.at[i], left_all.at[layer, col * held + i],
                      ly_send.at[i], ly_recv.at[i], twin_id)

    def twin_arrival(i):
        return remote(left_ref.at[i], left_all.at[other, col * held + i],
                      ly_send.at[i], ly_recv.at[i], twin_id)

    def left_copy(kind, i, slot):
        source, target = col, sibling_id
        if slot >= chips:
            source = peer_col(cols - slot + chips - 1)
        elif slot:
            target = peer_id(slot)
        at = (layer if kind == 0 else other), source * held + i
        src = left_ref.at[i] if kind == 0 and slot < chips else left_all.at[at]
        return remote(src, left_all.at[at], lc_send.at[kind, i, slot], lc_recv.at[kind, i, slot], target)

    def left_arrival(kind, i, slot):
        source = sibling
        if slot >= chips:
            source = lax.rem(sibling + 2 * (cols - slot + chips - 1), cols)
        elif slot:
            source = peer_col(cols - slot)
        at = (layer if kind == 0 else other), source * held + i
        return remote(left_all.at[at], left_all.at[at], lc_send.at[kind, i, slot],
                      lc_recv.at[kind, i, slot], sibling_id)

    def relay(kind):
        for i in range(held):
            for j in range(1, chips):
                left_arrival(kind, i, j).wait_recv()
                left_copy(kind, i, chips - 1 + j).start()

    for i in range(held):
        twin_copy(i).start()
    for way in ways:
        send_ring(way, 0, True)
    for i in range(held):
        for slot in range(chips - 1, -1, -1):
            left_copy(0, i, slot).start()
    for way in ways:
        send_ring(way, 1, True)

    for o in range(outs + 1):
        buf[cap + o] = jnp.zeros((bs, bs), jnp.float32)

    for copy in own_copies:
        copy.wait()
    remote(stacks_ref, lists.at[other], st_send, st_recv, twin_id).wait_recv()

    def gathered(entry):
        return jnp.concatenate([lists[0, entry], lists[1, entry]], axis=0)

    out_at = gathered(2) - layer * outs
    out_at = jnp.where((out_at >= 0) & (out_at < outs), out_at, outs)
    lane = lax.broadcasted_iota(jnp.int32, out_at.shape, 1)
    before = cap + out_at
    final = cap + jnp.minimum(lane, outs)
    for q in range(cap):
        mine = out_at[:, q:q + 1]
        before = jnp.where((out_at == mine) & (lane > q), q, before)
        final = jnp.where(lane == mine, q, final)
    tab_v[0, :, :cap] = gathered(1) * sa + gathered(0)
    tab_v[1, :, :cap] = before
    tab_v[2, :, :cap] = final
    tab_copy = pltpu.make_async_copy(tab_v, tab_s, tab_sem)
    tab_copy.start()

    for i in range(held):
        twin_arrival(i).wait_recv()
        for slot in range(chips - 1, -1, -1):
            left_copy(1, i, slot).start()
    tab_copy.wait()
    relay(0)

    def split(value):
        high = value.astype(jnp.bfloat16)
        return high, (value - high.astype(jnp.float32)).astype(jnp.bfloat16)

    def widen(spot):
        layer_at, row_at = unplace(spot)
        for a in range(sa):
            high, rest = split(left_all[layer_at, row_at, a])
            for n in range(4):
                wide[a * bs:(a + 1) * bs, n * bs:(n + 1) * bs] = rest if n % 2 else high

    def multiply(spot, b):
        parts = [split(right_all[spot, b + n]) for n in range(2)]
        deep = jnp.concatenate([parts[0][0], parts[1][0]], axis=1)
        low = jnp.concatenate([parts[0][1], parts[1][1]], axis=1)
        stacked = jnp.concatenate([deep, deep, low, low], axis=0)
        product = jnp.dot(wide[...], stacked, preferred_element_type=jnp.float32)
        for n in range(2):
            for a in range(sa):
                pairs[(b + n) * sa + a] = product[a * bs:(a + 1) * bs, n * bs:(n + 1) * bs]

    def gather_sums(spot, target, offset):
        layer_at, row_at = unplace(spot)
        at = layer_at * pieces + row_at

        def chain(q, carry):
            buf[q] = pairs[tab_s[0, at, q]] + buf[tab_s[1, at, q]]
            return carry

        lax.fori_loop(0, cap, chain, 0, unroll=8)

        def keep(o, carry):
            target[offset + o] = buf[tab_s[2, at, o]]
            return carry

        lax.fori_loop(0, outs, keep, 0, unroll=8)

    def accumulate(spot):
        widen(spot)
        for b in range(0, sb, 2):
            multiply(spot, b)
        gather_sums(spot, buf, cap)

    def pass_on(d, late):
        for way in ways:
            await_ring(way, 2 * d - 2 + late)

            @pl.when(d < rows - 1)
            def _():
                send_ring(way, 2 * d + late)

            @pl.when(d == rows - 1)
            def _():
                for u in ((2,) if late else (0, 1)):
                    send_end(way, u)

    pass_on(1, 0)
    relay(1)
    pass_on(1, 1)
    for kind in range(2):
        for i in range(held):
            for slot in (0,) + tuple(range(chips, cols - 1)):
                left_arrival(kind, i, slot).wait_recv()

    def first(j, carry):
        accumulate(wrap(me + j))
        return carry

    lax.fori_loop(0, 2, first, 0)

    def step(d, carry):
        pass_on(d, 0)
        accumulate(wrap(me - (d - 1)))
        pass_on(d, 1)
        accumulate(wrap(me + d))
        return carry

    lax.fori_loop(2, rows, step, 0)
    accumulate(wrap(me - (rows - 1)))
    opposite = wrap(me + rows)
    widen(opposite)
    stack_copy.wait_send()
    for i in range(held):
        twin_copy(i).wait_send()
        for kind in range(2):
            for slot in range(cols - 1):
                left_copy(kind, i, slot).wait_send()

    def drain(s, carry):
        for way in range(2):
            ring_copy(way, s, s // 2).wait_send()
        return carry

    lax.fori_loop(0, ring - 2, drain, 0)
    for t in (0, 3, 1, 2):
        await_end(t)
        for b in range(t * quarter, (t + 1) * quarter, 2):
            multiply(opposite, b)
    gather_sums(opposite, out_ref, 0)
    for way in range(2):
        for u in range(3):
            drain_end(way, u)


def body(rows, cols, left_blocks, right_blocks, pair_stacks):
    left_local = left_blocks[0, 0]
    right_local = right_blocks[0, 0, 0]
    stacks = jnp.swapaxes(pair_stacks[0, 0, 0], 0, 1)
    held, sa, bs, _ = left_local.shape
    sb = right_local.shape[0]
    _, pieces, cap = stacks.shape
    outs = OUT_TILE // 2
    f32 = jnp.float32
    dma = pltpu.SemaphoreType.DMA
    vmem = pl.BlockSpec(memory_space=pltpu.VMEM)
    block = bs * bs * 4
    blocks = 2 * pieces * (sa + sb) + sa * sb + cap + 2 * outs + sb + held * sa + 16
    result = pl.pallas_call(
        functools.partial(kernel, rows, cols),
        out_shape=jax.ShapeDtypeStruct((outs, bs, bs), f32),
        in_specs=[pl.BlockSpec(memory_space=pltpu.HBM)] * 3,
        out_specs=vmem,
        scratch_shapes=[
            pltpu.VMEM((2, pieces, sa, bs, bs), f32),
            pltpu.VMEM((2 * rows, sb, bs, bs), f32),
            pltpu.VMEM((2, 3, pieces, cap), jnp.int32),
            pltpu.VMEM((3, 2 * pieces, 128), jnp.int32),
            pltpu.SMEM((3, 2 * pieces, 128), jnp.int32),
            pltpu.VMEM((sa * sb, bs, bs), f32),
            pltpu.VMEM((sa * bs, 4 * bs), jnp.bfloat16),
            pltpu.VMEM((cap + outs + 1, bs, bs), f32),
            dma((2, 2 * rows - 2)),
            dma((2, 2 * rows - 2)),
            dma((2, 4)),
            dma((4,)),
            dma((held,)),
            dma((held,)),
            dma((2, held, cols - 1)),
            dma((2, held, cols - 1)),
            dma, dma, dma,
            dma((3,)),
        ],
        compiler_params=pltpu.CompilerParams(
            collective_id=0, has_side_effects=True, vmem_limit_bytes=blocks * block + (6 << 20)),
        name="ring_window",
    )(*(pltpu.with_memory_space_constraint(v, pltpu.HBM) for v in (left_local, right_local, stacks)))
    return result[None, None]


def solution(mesh):
    placed = (
        P("row", "layer", "col", None, None, None),
        P("layer", "row", "col", None, None, None),
        P("row", "col", "layer", None, None, None),
    )
    return jax.shard_map(
        functools.partial(body, mesh.shape["row"], mesh.shape["col"]),
        mesh=mesh,
        in_specs=placed,
        out_specs=P("row", "col", "layer", None, None),
        check_vma=False,
    )
```

time: 54.7 us -> 51.9 us (0.949); the launches traced: 53.9 us -> 51.8 us
  local copies, waits for them, and re-layouts: 3.65 us -> 0.97 us
  Pallas kernels: 50.2 us -> 50.8 us
    unnamed x7 -> x1, local copies, waits for them, and re-layouts: 3.65 us -> 0.97 us
    pallas_call x1, Pallas kernels: 50.2 us -> 50.8 us  [body(): pl.pallas_call(functools.partial(kernel, rows, cols), out_shape=jax.Shape...]
where the time goes in v3:
time: 51.9 us; the launch traced here: 51.8 us
  Pallas kernels  50.8 us (98%)
  local copies, waits for them, and re-layouts  0.97 us (2%)
    pallas_call x1, Pallas kernels, body(): pl.pallas_call(functools.partial(kernel, rows, cols), out_shape=jax.Shape...  50.8 us

profile of v3, /device:TPU:0, one launch (start us, length us, event | category | flops | bytes accessed | tf_op | source)
XLA Modules:
  0.0 51.8 jit_solution(13715685143901472545)
XLA Ops:
  0.0 50.8 %ring_window.1 = f32[16,128,128]{2,1,0:T(8,128)S(1)} custom-call(f32[1,4,128,128]{3,2,1,0:T(8,128)} %bitcast.8, f32[8,128,128]{2,1,0:T(8,128)} %bitcast.7, s32[3,4,32]{2,1,0:T(4,128)} %bitcast.9), custom_call_target="tpu_custom_call" | custom-call | tf_op jit(solution)/shard_map/ring_window/pallas_call | solution.py:321
  50.8 1.0 %copy.5 = f32[1,1,16,128,128]{4,3,2,1,0:T(8,128)} copy(f32[1,1,16,128,128]{4,3,2,1,0:T(8,128)S(1)} %bitcast.6) | data formatting | bytes 2097152

commit v4 on v3

--- a/solution.py
+++ b/solution.py
@@ -217,10 +217,10 @@
         deep = jnp.concatenate([parts[0][0], parts[1][0]], axis=1)
         low = jnp.concatenate([parts[0][1], parts[1][1]], axis=1)
         stacked = jnp.concatenate([deep, deep, low, low], axis=0)
-        product = jnp.dot(wide[...], stacked, preferred_element_type=jnp.float32)
-        for n in range(2):
-            for a in range(sa):
-                pairs[(b + n) * sa + a] = product[a * bs:(a + 1) * bs, n * bs:(n + 1) * bs]
+        for a in range(sa):
+            product = jnp.dot(wide[a * bs:(a + 1) * bs], stacked, preferred_element_type=jnp.float32)
+            for n in range(2):
+                pairs[(b + n) * sa + a] = product[:, n * bs:(n + 1) * bs]
 
     def gather_sums(spot, target, offset):
         layer_at, row_at = unplace(spot)
@@ -254,7 +254,7 @@
 
             @pl.when(d == rows - 1)
             def _():
-                for u in ((2,) if late else (0, 1)):
+                for u in ((1, 2) if late else (0,)):
                     send_end(way, u)
 
     pass_on(1, 0)

time: 51.9 us -> 51.5 us (level)
  no operation moved by 1% of the time
where the time goes in v4:
time: 51.5 us; the launch traced here: 51.4 us
  Pallas kernels  50.4 us (98%)
  local copies, waits for them, and re-layouts  0.97 us (2%)
    pallas_call x1, Pallas kernels, body(): pl.pallas_call(functools.partial(kernel, rows, cols), out_shape=jax.Shape...  50.4 us

profile of v4, /device:TPU:0, one launch (start us, length us, event | category | flops | bytes accessed | tf_op | source)
XLA Modules:
  0.0 51.4 jit_solution(18015880834132485065)
XLA Ops:
  0.0 50.4 %ring_window.1 = f32[16,128,128]{2,1,0:T(8,128)S(1)} custom-call(f32[1,4,128,128]{3,2,1,0:T(8,128)} %bitcast.8, f32[8,128,128]{2,1,0:T(8,128)} %bitcast.7, s32[3,4,32]{2,1,0:T(4,128)} %bitcast.9), custom_call_target="tpu_custom_call" | custom-call | tf_op jit(solution)/shard_map/ring_window/pallas_call | solution.py:321
  50.4 1.0 %copy.5 = f32[1,1,16,128,128]{4,3,2,1,0:T(8,128)} copy(f32[1,1,16,128,128]{4,3,2,1,0:T(8,128)S(1)} %bitcast.6) | data formatting | bytes 2097152
